TPU v7x, 32 devices: a whole 2x2x4 slice. The times are simulated.
32 devices in a mesh: blk: 8 (over z, x), rep: 4 (over y, core).
Axes of the slice: x: 2, y: 2, z: 4, core: 2. Of those that a mesh axis runs over, the one named last changes fastest.
Arguments:
- features: bfloat16 [32768, 128], P('blk'), may hold values from -6 to 6
- weight: bfloat16 [128, 256], replicated, may hold values from -0.5 to 0.5
- bias: float32 [256], replicated, may hold values from -3 to 3
- tile_values: bfloat16 [8, 8, 160, 128, 128], P('blk', 'rep'), may hold values from 0 to 0.041748047
- tile_place: int32 [8, 8, 160], P('blk', 'rep'), may hold values from 0 to 1023, as said below
- tile_count: int32 [8, 8], P('blk', 'rep'), may hold values from 1 to 160, as said below
Outputs:
- activations: bfloat16 [32768, 256], P('blk')
Inputs may be any that keep to these rules, and one draw needn't show every extreme that they name: `tile_place`: within one pair of destination block and section the 160 positions are distinct. `tile_count`: some pair of destination block and section has all 160 slots occupied.
All inputs are finite; a program needn't handle non-finite values.
Results may differ from a plain program's by a relative error of at most 0.0046.
Values may be sent and summed in bfloat16 or wider, within the bound.
A program may use at most 128 MiB of HBM per device.

v0:
```python
import jax
import jax.numpy as jnp
from jax import lax
from jax.sharding import PartitionSpec as P

TILE = 128


def section_terms(source, tiles, place, count):
    row_count = source.shape[0]
    row_tiles = row_count // TILE
    column = place % row_tiles
    target = place // row_tiles
    blocked = source.reshape(row_tiles, TILE, source.shape[1])
    pieces = jnp.take(blocked, column, axis=0)
    products = jnp.einsum("kij,kjf->kif", tiles, pieces, preferred_element_type=jnp.float32)
    slot_ids = jnp.arange(place.shape[0], dtype=jnp.int32)
    live = (slot_ids < count).astype(jnp.float32)
    products = products * live[:, None, None]
    summed = jax.ops.segment_sum(products, target, num_segments=row_tiles)
    return summed.reshape(row_count, source.shape[1])


def shards(features, weight, bias, tile_values, tile_place, tile_count):
    row_count = features.shape[0]
    sections = tile_values.shape[1]
    cycle_size = lax.axis_size("blk")
    my_replica = lax.axis_index("rep")
    partial_value = jnp.zeros((row_count, features.shape[1]), jnp.float32)
    piece_rows = row_count // cycle_size
    pieces = features.reshape(cycle_size, piece_rows, features.shape[1])
    holding = lax.all_to_all(pieces, "blk", split_axis=0, concat_axis=0, tiled=True)
    for section_index in range(sections):
        offset = my_replica * sections + section_index
        rolled = jnp.roll(holding, offset, axis=0)
        arrived = lax.all_to_all(rolled, "blk", split_axis=0, concat_axis=0, tiled=True)
        source = arrived.reshape(row_count, features.shape[1])
        partial_value = partial_value + section_terms(
            source,
            tile_values[0, section_index],
            tile_place[0, section_index],
            tile_count[0, section_index],
        )
    summed = lax.psum(partial_value, "rep")
    aggregated = summed.astype(jnp.bfloat16)
    output = jnp.dot(aggregated, weight, preferred_element_type=jnp.float32) + bias
    return jnp.maximum(output, 0.0).astype(jnp.bfloat16)


def solution(mesh):
    in_specs = (
        P("blk", None),
        P(),
        P(),
        P("blk", "rep", None, None, None),
        P("blk", "rep", None),
        P("blk", "rep"),
    )
    out_specs = P("blk", None)
    return jax.shard_map(shards, mesh=mesh, in_specs=in_specs, out_specs=out_specs, check_vma=False)
```

profile of v0, /device:TPU:1, one launch (start us, length us, event | category | flops | bytes accessed | tf_op | source)
XLA Modules:
  0.0 222.3 jit_solution(2415213686946378558)
XLA Ops:
  0.0 0.0 copy-start
  0.0 6.5 %all-to-all-start = ((bf16[8,512,128]{2,1,0:T(8,128)(2,1)}), bf16[8,512,128]{2,1,0:T(8,128)(2,1)S(1)}, u32[]{:S(2)}, u32[]{:S(2)}) async-start(bf16[8,512,128]{2,1,0:T(8,128)(2,1)} %bitcast.45), calls=%async_computation | async-start | bytes 2097152 | tf_op jit(solution)/shard_map/all_to_all | solution.py:32
  6.5 25.0 %all-to-all-done = bf16[8,512,128]{2,1,0:T(8,128)(2,1)S(1)} async-done(((bf16[8,512,128]{2,1,0:T(8,128)(2,1)}), bf16[8,512,128]{2,1,0:T(8,128)(2,1)S(1)}, u32[]{:S(2)}, u32[]{:S(2)}) %all-to-all-start) | async-done | bytes 1048608 | tf_op jit(solution)/shard_map/all_to_all | solution.py:32
  31.4 0.1 constant_dynamic-update-slice_fusion.1
  31.5 0.0 copy-start.2
  31.5 0.0 copy-start.3
  31.5 0.1 constant_dynamic-update-slice_fusion
  31.7 1.1 constant_dynamic-slice_fusion
  32.8 29.1 %all_to_all.15 = bf16[8,512,128]{2,1,0:T(8,128)(2,1)S(1)} all-to-all(bf16[8,512,128]{2,1,0:T(8,128)(2,1)S(1)} %get-tuple-element.11), channel_id=1, replica_groups=mesh['blk'=8,'rep'=4] {'blk'}, dimensions={0} | all-to-all | bytes 2097152 | tf_op jit(solution)/shard_map/all_to_all | solution.py:36
  61.9 4.3 %all-to-all-start.1 = ((bf16[8,512,128]{2,1,0:T(8,128)(2,1)}), bf16[8,512,128]{2,1,0:T(8,128)(2,1)S(1)}, u32[]{:S(2)}, u32[]{:S(2)}) async-start(bf16[8,512,128]{2,1,0:T(8,128)(2,1)} %get-tuple-element.12), calls=%async_computation.1 | async-start | bytes 2097152 | tf_op jit(solution)/shard_map/all_to_all | solution.py:36
  66.2 0.0 copy-done.2
  66.2 0.0 copy-done.3
  66.2 0.7 fusion.28
  66.9 0.7 compare_and_fusion
  67.6 0.6 compare_and_fusion.1
  68.2 7.7 %gather_fusion.1 = bf16[160,128,128]{2,1,0:T(8,128)(2,1)} fusion(bf16[32,128,128]{2,1,0:T(8,128)(2,1)S(1)} %bitcast.43, s32[1024]{0:T(1024)S(1)} %pad_clamp_fusion), kind=kCustom, calls=%fused_computation.1.clone | custom fusion | bytes 10486400 | tf_op jit(solution)/shard_map/jit(_take)/gather | solution.py:15
  75.9 11.8 %multiply_bitcast_fusion = f32[160,128,128]{1,2,0:T(8,128)} fusion(f32[160]{0:T(256)S(1)} %get-tuple-element.20, bf16[1,2,160,128,128]{4,3,2,1,0:T(8,128)(2,1)} %param.13, bf16[160,128,128]{2,1,0:T(8,128)(2,1)} %gather_fusion.1, pred[160]{0:T(512)(128)(4,1)S(1)} %get-tuple-element.6), kind=kOutput, calls=%fused_computation.4 | convolution fusion | flops 676331520 | bytes 20972320 | tf_op jit(solution)/shard_map/kij,kjf->kif/dot_general | solution.py:16
  87.7 11.7 %copy.12 = f32[160,128,128]{2,1,0:T(8,128)} copy(f32[160,128,128]{1,2,0:T(8,128)} %multiply_bitcast_fusion) | data formatting | bytes 20971520 | tf_op jit(solution)/shard_map/mul | solution.py:19
  99.5 0.0 all-to-all-done.1
  99.5 7.7 %gather_fusion = bf16[160,128,128]{2,1,0:T(8,128)(2,1)} fusion(bf16[32,128,128]{2,1,0:T(8,128)(2,1)S(1)} %bitcast.42, s32[1024]{0:T(1024)S(1)} %pad_clamp_fusion.1), kind=kCustom, calls=%fused_computation.clone | custom fusion | bytes 10486400 | tf_op jit(solution)/shard_map/jit(_take)/gather | solution.py:15
  107.2 11.8 %multiply_bitcast_fusion.1 = f32[160,128,128]{1,2,0:T(8,128)} fusion(f32[160]{0:T(256)S(1)} %get-tuple-element.19, bf16[1,2,160,128,128]{4,3,2,1,0:T(8,128)(2,1)} %param.13, bf16[160,128,128]{2,1,0:T(8,128)(2,1)} %gather_fusion, pred[160]{0:T(512)(128)(4,1)S(1)} %get-tuple-element.9), kind=kOutput, calls=%fused_computation.5 | convolution fusion | flops 676331520 | bytes 20972320 | tf_op jit(solution)/shard_map/kij,kjf->kif/dot_general | solution.py:16
  119.0 11.7 %copy.10 = f32[160,128,128]{2,1,0:T(8,128)} copy(f32[160,128,128]{1,2,0:T(8,128)} %multiply_bitcast_fusion.1) | data formatting | bytes 20971520 | tf_op jit(solution)/shard_map/mul | solution.py:19
  130.7 0.2 broadcast.127.clone.1
  131.0 21.2 %scatter_fusion.1 = f32[32,128,128]{2,1,0:T(8,128)S(1)} fusion(f32[32,128,128]{2,1,0:T(8,128)S(1)} %broadcast.127.clone.1, s32[160]{0:T(256)S(1)} %bitcast.47, f32[160,128,128]{2,1,0:T(8,128)} %copy.12), kind=kCustom, calls=%fused_computation.3 | custom fusion | flops 2621440 | bytes 31457920 | tf_op jit(solution)/shard_map/scatter-add | solution.py:20
  152.2 0.0 copy-start.1
  152.2 1.3 copy-done.1
  153.5 0.2 broadcast.127.clone
  153.7 21.2 %scatter_fusion = f32[32,128,128]{2,1,0:T(8,128)S(1)} fusion(f32[32,128,128]{2,1,0:T(8,128)S(1)} %broadcast.127.clone, s32[160]{0:T(256)S(1)} %bitcast.46, f32[160,128,128]{2,1,0:T(8,128)} %copy.10), kind=kCustom, calls=%fused_computation.2 | custom fusion | flops 2621440 | bytes 31457920 | tf_op jit(solution)/shard_map/scatter-add | solution.py:20
  174.9 0.0 copy-start.4
  174.9 3.2 %add.66 = f32[32,128,128]{2,1,0:T(8,128)} add(f32[32,128,128]{2,1,0:T(8,128)S(1)} %scatter_fusion, f32[32,128,128]{2,1,0:T(8,128)} %copy-done.1) | non-fusion elementwise | flops 524288 | bytes 6291456 | tf_op jit(solution)/shard_map/add | solution.py:38
  178.1 42.2 %all-reduce.1 = bf16[4096,128]{1,0:T(8,128)(2,1)S(1)} all-reduce(f32[4096,128]{1,0:T(8,128)} %bitcast.44), channel_id=1, replica_groups=mesh['blk'=8,'rep'=4] {'rep'}, use_global_device_ids=true, to_apply=%region_2.5 | all-reduce | flops 524288 | bytes 3145728 | tf_op jit(solution)/shard_map/psum | solution.py:44
  220.3 0.0 copy-done
  220.3 0.0 copy-done.4
  220.3 2.0 fusion.11
  (4 shorter events, 0.0 us)
Async XLA Ops:
  0.0 220.3 %copy-start = (bf16[128,256]{1,0:T(8,128)(2,1)S(1)}, bf16[128,256]{1,0:T(8,128)(2,1)}, u32[]{:S(2)}) copy-start(bf16[128,256]{1,0:T(8,128)(2,1)} %param.11) | copy-start | bytes 196612
  0.0 31.4 %all-to-all-start = ((bf16[8,512,128]{2,1,0:T(8,128)(2,1)}), bf16[8,512,128]{2,1,0:T(8,128)(2,1)S(1)}, u32[]{:S(2)}, u32[]{:S(2)}) async-start(bf16[8,512,128]{2,1,0:T(8,128)(2,1)} %bitcast.45), calls=%async_computation | async-start | bytes 2097152 | tf_op jit(solution)/shard_map/all_to_all | solution.py:32
  31.5 34.7 %copy-start.2 = (s32[1,2,160]{2,1,0:T(2,128)S(1)}, s32[1,2,160]{2,1,0:T(2,128)}, u32[]{:S(2)}) copy-start(s32[1,2,160]{2,1,0:T(2,128)} %param.14) | copy-start | bytes 3844
  31.5 34.7 %copy-start.3 = (s32[1,2]{1,0:T(1,128)S(1)}, s32[1,2]{1,0:T(1,128)}, u32[]{:S(2)}) copy-start(s32[1,2]{1,0:T(1,128)} %param.15) | copy-start | bytes 28
  61.9 37.5 %all-to-all-start.1 = ((bf16[8,512,128]{2,1,0:T(8,128)(2,1)}), bf16[8,512,128]{2,1,0:T(8,128)(2,1)S(1)}, u32[]{:S(2)}, u32[]{:S(2)}) async-start(bf16[8,512,128]{2,1,0:T(8,128)(2,1)} %get-tuple-element.12), calls=%async_computation.1 | async-start | bytes 2097152 | tf_op jit(solution)/shard_map/all_to_all | solution.py:36
  152.2 1.3 copy-start.1
  174.9 45.4 %copy-start.4 = (f32[256]{0:T(256)S(1)}, f32[256]{0:T(256)}, u32[]{:S(2)}) copy-start(f32[256]{0:T(256)} %param.12) | copy-start | bytes 3076
where the time goes:
time: 224 us; the launch traced here: 222 us
  blocking collectives  71.3 us (32%)
  other arithmetic  46.8 us (21%)
  local copies, waits for them, and re-layouts  42.7 us (19%)
  matrix products  25.7 us (11%)
  waiting for transfers between devices  25 us (11%)
  starting transfers between devices  10.7 us (5%)
    scatter-add x2, other arithmetic, section_terms(): summed = jax.ops.segment_sum(products, target, num_segments=row_tiles)  42.4 us
    psum x1, blocking collectives, shards(): summed = lax.psum(partial_value, 'rep')  42.2 us
    all_to_all x1, blocking collectives, shards(): lax.all_to_all(rolled, 'blk', split_axis=0, concat_axis=0, tiled=True)  29.1 us
    all_to_all x1, waiting for transfers between devices, shards(): lax.all_to_all(pieces, 'blk', split_axis=0, concat_axis=0, tiled=True)  25 us
    dot_general x2, matrix products, section_terms(): jnp.einsum('kij,kjf->kif', tiles, pieces, preferred_element_type=jnp.floa...  23.6 us
    mul x2, local copies, waits for them, and re-layouts, section_terms(): products = products * live[:, None, None]  23.5 us
    gather x2, local copies, waits for them, and re-layouts, section_terms(): pieces = jnp.take(blocked, column, axis=0)  15.4 us
    all_to_all x1, starting transfers between devices, shards(): lax.all_to_all(pieces, 'blk', split_axis=0, concat_axis=0, tiled=True)  6.47 us
  transfers between devices with their start and end apart: 2, of which 1 were waited for; matrix products, arithmetic and copies ran while one was open for 15% of the time, Pallas kernels for 0%

commit v1 on v0

--- a/solution.py
+++ b/solution.py
@@ -4,6 +4,15 @@
 from jax.sharding import PartitionSpec as P
 
 TILE = 128
+
+
+def doubling_sum(x, axis):
+    peers = lax.axis_size(axis)
+    acc, hop = (x, 1)
+    while hop < peers:
+        acc = acc + lax.ppermute(acc, axis, [(i, i ^ hop) for i in range(peers)])
+        hop = 2 * hop
+    return acc
 
 
 def section_terms(source, tiles, place, count):
@@ -41,7 +50,7 @@
             tile_place[0, section_index],
             tile_count[0, section_index],
         )
-    summed = lax.psum(partial_value, "rep")
+    summed = doubling_sum(partial_value, "rep")
     aggregated = summed.astype(jnp.bfloat16)
     output = jnp.dot(aggregated, weight, preferred_element_type=jnp.float32) + bias
     return jnp.maximum(output, 0.0).astype(jnp.bfloat16)

time: 224 us -> 234 us (1.045)
  waiting for transfers between devices: 25 us -> 74.3 us
  blocking collectives: 71.3 us -> 29.1 us
  starting transfers between devices: 10.7 us -> 13.4 us
    ppermute x0 -> x2, waiting for transfers between devices: none -> 49.4 us  [doubling_sum(): acc = acc + lax.ppermute(acc, axis, [(i, i ^ hop) for i in range(peers)])]
    psum x1 -> x0, blocking collectives: 42.2 us -> none  [shards(): summed = lax.psum(partial_value, 'rep')]
    ppermute x0 -> x2, starting transfers between devices: none -> 2.68 us  [doubling_sum(): acc = acc + lax.ppermute(acc, axis, [(i, i ^ hop) for i in range(peers)])]
  transfers between devices with their start and end apart: 2 -> 4, of which waited for: 1 -> 3; matrix products, arithmetic and copies ran while one was open for 15% -> 14% of each run, Pallas kernels for 0% -> 0%
where the time goes in v1:
time: 234 us; the launch traced here: 231 us
  waiting for transfers between devices  74.3 us (32%)
  other arithmetic  45.7 us (20%)
  local copies, waits for them, and re-layouts  42.6 us (18%)
  blocking collectives  29.1 us (12%)
  matrix products  25.7 us (11%)
  starting transfers between devices  13.4 us (6%)
    ppermute x2, waiting for transfers between devices, doubling_sum(): acc = acc + lax.ppermute(acc, axis, [(i, i ^ hop) for i in range(peers)])  49.4 us
    scatter-add x2, other arithmetic, section_terms(): summed = jax.ops.segment_sum(products, target, num_segments=row_tiles)  42.4 us
    all_to_all x1, blocking collectives, shards(): lax.all_to_all(rolled, 'blk', split_axis=0, concat_axis=0, tiled=True)  29.1 us
    all_to_all x1, waiting for transfers between devices, shards(): lax.all_to_all(pieces, 'blk', split_axis=0, concat_axis=0, tiled=True)  25 us
    dot_general x2, matrix products, section_terms(): jnp.einsum('kij,kjf->kif', tiles, pieces, preferred_element_type=jnp.floa...  23.7 us
    mul x2, local copies, waits for them, and re-layouts, section_terms(): products = products * live[:, None, None]  23.5 us
    gather x2, local copies, waits for them, and re-layouts, section_terms(): pieces = jnp.take(blocked, column, axis=0)  15.4 us
    all_to_all x1, starting transfers between devices, shards(): lax.all_to_all(pieces, 'blk', split_axis=0, concat_axis=0, tiled=True)  6.47 us
  transfers between devices with their start and end apart: 4, of which 3 were waited for; matrix products, arithmetic and copies ran while one was open for 14% of the time, Pallas kernels for 0%

profile of v1, /device:TPU:1, one launch (start us, length us, event | category | flops | bytes accessed | tf_op | source)
XLA Modules:
  0.0 231.1 jit_solution(1260529867881614547)
XLA Ops:
  0.0 0.0 copy-start
  0.0 6.5 %all-to-all-start = ((bf16[8,512,128]{2,1,0:T(8,128)(2,1)}), bf16[8,512,128]{2,1,0:T(8,128)(2,1)S(1)}, u32[]{:S(2)}, u32[]{:S(2)}) async-start(bf16[8,512,128]{2,1,0:T(8,128)(2,1)} %bitcast.45), calls=%async_computation | async-start | bytes 2097152 | tf_op jit(solution)/shard_map/all_to_all | solution.py:41
  6.5 25.0 %all-to-all-done = bf16[8,512,128]{2,1,0:T(8,128)(2,1)S(1)} async-done(((bf16[8,512,128]{2,1,0:T(8,128)(2,1)}), bf16[8,512,128]{2,1,0:T(8,128)(2,1)S(1)}, u32[]{:S(2)}, u32[]{:S(2)}) %all-to-all-start) | async-done | bytes 1048608 | tf_op jit(solution)/shard_map/all_to_all | solution.py:41
  31.4 0.1 constant_dynamic-update-slice_fusion.1
  31.5 0.0 copy-start.2
  31.5 0.0 copy-start.3
  31.5 0.1 constant_dynamic-update-slice_fusion
  31.7 1.1 constant_dynamic-slice_fusion
  32.8 29.1 %all_to_all.15 = bf16[8,512,128]{2,1,0:T(8,128)(2,1)S(1)} all-to-all(bf16[8,512,128]{2,1,0:T(8,128)(2,1)S(1)} %get-tuple-element.11), channel_id=1, replica_groups=mesh['blk'=8,'rep'=4] {'blk'}, dimensions={0} | all-to-all | bytes 2097152 | tf_op jit(solution)/shard_map/all_to_all | solution.py:45
  61.9 4.3 %all-to-all-start.1 = ((bf16[8,512,128]{2,1,0:T(8,128)(2,1)}), bf16[8,512,128]{2,1,0:T(8,128)(2,1)S(1)}, u32[]{:S(2)}, u32[]{:S(2)}) async-start(bf16[8,512,128]{2,1,0:T(8,128)(2,1)} %get-tuple-element.12), calls=%async_computation.1 | async-start | bytes 2097152 | tf_op jit(solution)/shard_map/all_to_all | solution.py:45
  66.2 0.0 copy-done.2
  66.2 0.0 copy-done.3
  66.2 0.6 fusion.27
  66.9 0.6 compare_and_fusion
  67.5 0.6 compare_and_fusion.1
  68.2 7.7 %gather_fusion.1 = bf16[160,128,128]{2,1,0:T(8,128)(2,1)} fusion(bf16[32,128,128]{2,1,0:T(8,128)(2,1)S(1)} %bitcast.43, s32[1024]{0:T(1024)S(1)} %pad_clamp_fusion), kind=kCustom, calls=%fused_computation.1.clone | custom fusion | bytes 10486400 | tf_op jit(solution)/shard_map/jit(_take)/gather | solution.py:24
  75.9 11.8 %multiply_bitcast_fusion = f32[160,128,128]{1,2,0:T(8,128)} fusion(f32[160]{0:T(256)S(1)} %get-tuple-element.20, bf16[1,2,160,128,128]{4,3,2,1,0:T(8,128)(2,1)} %param.13, bf16[160,128,128]{2,1,0:T(8,128)(2,1)} %gather_fusion.1, pred[160]{0:T(512)(128)(4,1)S(1)} %get-tuple-element.6), kind=kOutput, calls=%fused_computation.4 | convolution fusion | flops 676331520 | bytes 20972320 | tf_op jit(solution)/shard_map/kij,kjf->kif/dot_general | solution.py:25
  87.7 11.7 %copy.12 = f32[160,128,128]{2,1,0:T(8,128)} copy(f32[160,128,128]{1,2,0:T(8,128)} %multiply_bitcast_fusion) | data formatting | bytes 20971520 | tf_op jit(solution)/shard_map/mul | solution.py:28
  99.4 0.0 all-to-all-done.1
  99.4 7.7 %gather_fusion = bf16[160,128,128]{2,1,0:T(8,128)(2,1)} fusion(bf16[32,128,128]{2,1,0:T(8,128)(2,1)S(1)} %bitcast.42, s32[1024]{0:T(1024)S(1)} %pad_clamp_fusion.1), kind=kCustom, calls=%fused_computation.clone | custom fusion | bytes 10486400 | tf_op jit(solution)/shard_map/jit(_take)/gather | solution.py:24
  107.2 11.8 %multiply_bitcast_fusion.1 = f32[160,128,128]{1,2,0:T(8,128)} fusion(f32[160]{0:T(256)S(1)} %get-tuple-element.19, bf16[1,2,160,128,128]{4,3,2,1,0:T(8,128)(2,1)} %param.13, bf16[160,128,128]{2,1,0:T(8,128)(2,1)} %gather_fusion, pred[160]{0:T(512)(128)(4,1)S(1)} %get-tuple-element.9), kind=kOutput, calls=%fused_computation.5 | convolution fusion | flops 676331520 | bytes 20972320 | tf_op jit(solution)/shard_map/kij,kjf->kif/dot_general | solution.py:25
  119.0 11.7 %copy.10 = f32[160,128,128]{2,1,0:T(8,128)} copy(f32[160,128,128]{1,2,0:T(8,128)} %multiply_bitcast_fusion.1) | data formatting | bytes 20971520 | tf_op jit(solution)/shard_map/mul | solution.py:28
  130.7 0.2 broadcast.127.clone.1
  131.0 21.2 %scatter_fusion.1 = f32[32,128,128]{2,1,0:T(8,128)S(1)} fusion(f32[32,128,128]{2,1,0:T(8,128)S(1)} %broadcast.127.clone.1, s32[160]{0:T(256)S(1)} %bitcast.47, f32[160,128,128]{2,1,0:T(8,128)} %copy.12), kind=kCustom, calls=%fused_computation.3 | custom fusion | flops 2621440 | bytes 31457920 | tf_op jit(solution)/shard_map/scatter-add | solution.py:29
  152.1 0.0 copy-start.1
  152.2 1.3 copy-done.1
  153.5 0.2 broadcast.127.clone
  153.7 21.2 %scatter_fusion = f32[32,128,128]{2,1,0:T(8,128)S(1)} fusion(f32[32,128,128]{2,1,0:T(8,128)S(1)} %broadcast.127.clone, s32[160]{0:T(256)S(1)} %bitcast.46, f32[160,128,128]{2,1,0:T(8,128)} %copy.10), kind=kCustom, calls=%fused_computation.2 | custom fusion | flops 2621440 | bytes 31457920 | tf_op jit(solution)/shard_map/scatter-add | solution.py:29
  174.9 0.0 copy-start.4
  174.9 1.8 add.70
  176.8 1.4 collective-permute-start
  178.1 3.8 %collective-permute-done = f32[4096,128]{1,0:T(8,128)S(1)} collective-permute-done((f32[4096,128]{1,0:T(8,128)S(1)}, f32[4096,128]{1,0:T(8,128)S(1)}, u32[]{:S(2)}, u32[]{:S(2)}) %collective-permute-start) | collective-permute-done | bytes 2097184 | tf_op jit(solution)/shard_map/ppermute | solution.py:13
  181.9 0.2 bitcast_add_fusion
  182.1 1.3 collective-permute-start.1
  183.4 45.6 %collective-permute-done.1 = f32[4096,128]{1,0:T(8,128)S(1)} collective-permute-done((f32[4096,128]{1,0:T(8,128)S(1)}, f32[4096,128]{1,0:T(8,128)S(1)}, u32[]{:S(2)}, u32[]{:S(2)}) %collective-permute-start.1) | collective-permute-done | bytes 2097184 | tf_op jit(solution)/shard_map/ppermute | solution.py:13
  229.0 0.0 copy-done
  229.0 0.0 copy-done.4
  229.0 2.0 fusion.11
  (4 shorter events, 0.0 us)
Async XLA Ops:
  0.0 229.0 %copy-start = (bf16[128,256]{1,0:T(8,128)(2,1)S(1)}, bf16[128,256]{1,0:T(8,128)(2,1)}, u32[]{:S(2)}) copy-start(bf16[128,256]{1,0:T(8,128)(2,1)} %param.11) | copy-start | bytes 196612
  0.0 31.4 %all-to-all-start = ((bf16[8,512,128]{2,1,0:T(8,128)(2,1)}), bf16[8,512,128]{2,1,0:T(8,128)(2,1)S(1)}, u32[]{:S(2)}, u32[]{:S(2)}) async-start(bf16[8,512,128]{2,1,0:T(8,128)(2,1)} %bitcast.45), calls=%async_computation | async-start | bytes 2097152 | tf_op jit(solution)/shard_map/all_to_all | solution.py:41
  31.5 34.7 %copy-start.2 = (s32[1,2,160]{2,1,0:T(2,128)S(1)}, s32[1,2,160]{2,1,0:T(2,128)}, u32[]{:S(2)}) copy-start(s32[1,2,160]{2,1,0:T(2,128)} %param.14) | copy-start | bytes 3844
  31.5 34.7 %copy-start.3 = (s32[1,2]{1,0:T(1,128)S(1)}, s32[1,2]{1,0:T(1,128)}, u32[]{:S(2)}) copy-start(s32[1,2]{1,0:T(1,128)} %param.15) | copy-start | bytes 28
  61.9 37.5 %all-to-all-start.1 = ((bf16[8,512,128]{2,1,0:T(8,128)(2,1)}), bf16[8,512,128]{2,1,0:T(8,128)(2,1)S(1)}, u32[]{:S(2)}, u32[]{:S(2)}) async-start(bf16[8,512,128]{2,1,0:T(8,128)(2,1)} %get-tuple-element.12), calls=%async_computation.1 | async-start | bytes 2097152 | tf_op jit(solution)/shard_map/all_to_all | solution.py:45
  152.1 1.3 copy-start.1
  174.9 54.1 %copy-start.4 = (f32[256]{0:T(256)S(1)}, f32[256]{0:T(256)}, u32[]{:S(2)}) copy-start(f32[256]{0:T(256)} %param.12) | copy-start | bytes 3076
  176.8 5.2 %collective-permute-start = (f32[4096,128]{1,0:T(8,128)S(1)}, f32[4096,128]{1,0:T(8,128)S(1)}, u32[]{:S(2)}, u32[]{:S(2)}) collective-permute-start(f32[4096,128]{1,0:T(8,128)S(1)} %bitcast.44), channel_id=1, source_target_pairs={{0,1},{1,0},{2,3},{3,2},{4,5},{5,4},{6,7},{7,6},{8,9},{9,8},{10,11... | collective-permute-start | bytes 6291464 | tf_op jit(solution)/shard_map/ppermute | solution.py:13
  182.1 46.9 %collective-permute-start.1 = (f32[4096,128]{1,0:T(8,128)S(1)}, f32[4096,128]{1,0:T(8,128)S(1)}, u32[]{:S(2)}, u32[]{:S(2)}) collective-permute-start(f32[4096,128]{1,0:T(8,128)S(1)} %bitcast_add_fusion), channel_id=1, source_target_pairs={{0,2},{1,3},{2,0},{3,1},{4,6},{5,7},{6,4},{7,5},{8,10},{9,11},{10,... | collective-permute-start | bytes 6291464 | tf_op jit(solution)/shard_map/ppermute | solution.py:13
